TPU v7x, 32 devices: a whole 2x2x4 slice. The times are simulated.
32 devices in a mesh: req: 4 (over z), tok: 8 (over y, x, core).
Axes of the slice: x: 2, y: 2, z: 4, core: 2. Of those that a mesh axis runs over, the one named last changes fastest.
Arguments:
- hidden_in: bfloat16 [4096, 2048], P(('req', 'tok')), may hold values from -1.5 to 1.5
- suffix_len: int32 [4, 4], P('req'), may hold values from 1 to 512, 1024 in all within a row
- prefix_of: int32 [4, 4], P('req'), may hold values from 0 to 3
- prefix_slot: int32 [4], replicated, may hold values from 0 to 3, each once
- prefix_cache: bfloat16 [4, 4, 2048, 128], P('req', None, 'tok'), may hold values from -160 to 160
- attn_gain: bfloat16 [2048], replicated, may hold values from 0.099609375 to 1.8984375
- query_weight: bfloat16 [2048, 2048], P(None, 'tok'), may hold values from -0.125 to 0.125
- keyval_weight: bfloat16 [4, 2048, 128], replicated, may hold values from -0.125 to 0.125
- out_weight: bfloat16 [2048, 2048], P('tok'), may hold values from -0.125 to 0.125
- mlp_gain: bfloat16 [2048], replicated, may hold values from 0.099609375 to 1.8984375
- gate_weight: bfloat16 [2048, 4096], P(None, 'req'), may hold values from -0.125 to 0.125
- up_weight: bfloat16 [2048, 4096], P(None, 'req'), may hold values from -0.125 to 0.125
- down_weight: bfloat16 [4096, 2048], P('req'), may hold values from -0.09375 to 0.09375
- final_gain: bfloat16 [2048], replicated, may hold values from 0.099609375 to 1.8984375
- head_weight: bfloat16 [32000, 2048], P('tok'), may hold values from -7 to 7
Outputs:
- hidden_out: bfloat16 [4096, 2048], P(('req', 'tok'))
- suffix_cache: bfloat16 [4096, 512], P('req', 'tok')
- last_rms: float32 [4, 4], P('req')
- top_logit: float32 [4, 4], P('req')
- log_total: float32 [4, 4], P('req')
Inputs may be any that keep to these rules, and one draw needn't show every extreme that they name: `suffix_len`: each owner's 4 lengths sum to 1024, and the largest of each owner is 512.
All inputs are finite; a program needn't handle non-finite values.
Results may differ from a plain program's by a relative error of at most 0.02.
Values may be sent and summed in bfloat16 or wider, within the bound.
A program may use at most 128 MiB of HBM per device.

v0:
```python
import math
import jax
import jax.numpy as jnp
from jax import lax
from jax.sharding import PartitionSpec as P

HD = 64
PRE_LEN = 16384
epsilon = 1e-05
neg_large = -1e30


def rms_scale(values, gain_vec):
    widened = values.astype(jnp.float32)
    mean_square = jnp.mean(widened * widened, axis=-1, keepdims=True)
    return widened * lax.rsqrt(mean_square + epsilon) * gain_vec.astype(jnp.float32)


def rotate(vectors, positions):
    half_width = vectors.shape[-1] // 2
    levels = jnp.arange(half_width).astype(jnp.float32)
    inverse = jnp.exp(levels * (-2.0 * math.log(10000.0) / vectors.shape[-1]))
    angles = positions.astype(jnp.float32)[:, None] * inverse[None, :]
    cosine = jnp.cos(angles)[:, None, :]
    sine_part = jnp.sin(angles)[:, None, :]
    first_half = vectors[..., :half_width]
    second_half = vectors[..., half_width:]
    return jnp.concatenate(
        [
            first_half * cosine - second_half * sine_part,
            second_half * cosine + first_half * sine_part,
        ],
        axis=-1,
    )


def owner_layout(lengths, row_count):
    end_rows = jnp.cumsum(lengths)
    starts = end_rows - lengths
    row_index = jnp.arange(row_count)
    member = (row_index[:, None] >= starts[None, :]) & (row_index[:, None] < end_rows[None, :])
    offsets = row_index - jnp.sum(jnp.where(member, starts[None, :], 0), axis=1)
    return (starts, end_rows, offsets)


def slot_lookup(chosen, prefix_slot):
    table_index = jnp.arange(prefix_slot.shape[0])
    hits = chosen[:, None] == table_index[None, :]
    return jnp.sum(jnp.where(hits, prefix_slot[None, :], 0), axis=1)


def request_attention(query_block, suffix_block, window, live_len):
    row_count = query_block.shape[0]
    head_width = query_block.shape[-1]
    window_len = window.shape[1]
    suffix_major = jnp.transpose(suffix_block, (1, 0, 2))
    key_rows = jnp.concatenate([window[:, :, :head_width], suffix_major[:, :, :head_width]], axis=1)
    value_rows = jnp.concatenate(
        [window[:, :, head_width:], suffix_major[:, :, head_width:]], axis=1
    )
    scores = jnp.einsum(
        "rgke,gse->gkrs", query_block, key_rows, preferred_element_type=jnp.float32
    ) * head_width ** (-0.5)
    row_index = jnp.arange(row_count)
    prefix_seen = jnp.arange(window_len)[None, :] > row_index[:, None]
    suffix_seen = (
        (row_index[None, :] <= row_index[:, None])
        & (row_index[:, None] - row_index[None, :] < window_len)
        & (row_index[None, :] < live_len)
    )
    visible = jnp.concatenate([prefix_seen, suffix_seen], axis=1)
    masked = jnp.where(visible, scores, neg_large)
    highest = jnp.max(masked, axis=-1, keepdims=True)
    weights = jnp.where(visible, jnp.exp(masked - highest), 0.0)
    totals = jnp.sum(weights, axis=-1, keepdims=True)
    totals = jnp.where(row_index[:, None] < live_len, totals, 1.0)
    rounded = weights.astype(jnp.bfloat16)
    mixed_rows = jnp.einsum(
        "gkrs,gse->rgke", rounded, value_rows, preferred_element_type=jnp.float32
    )
    mixed_rows = mixed_rows / jnp.transpose(totals, (2, 0, 1, 3))
    return mixed_rows.reshape(row_count, -1).astype(jnp.bfloat16)


def shards(
    hidden_in,
    suffix_len,
    prefix_of,
    prefix_slot,
    prefix_cache,
    attn_gain,
    query_weight,
    keyval_weight,
    out_weight,
    mlp_gain,
    gate_weight,
    up_weight,
    down_weight,
    final_gain,
    head_weight,
):
    tok_count = lax.axis_size("tok")
    tok_place = lax.axis_index("tok")
    tok_rows = hidden_in.shape[0]
    own_rows = tok_rows * tok_count
    most_rows = own_rows // 2
    heads_here = query_weight.shape[1] // HD
    kv_count = keyval_weight.shape[0]
    kv_head = tok_place * kv_count // tok_count
    repeat_count = tok_count // kv_count
    lengths = suffix_len[0]
    starts, end_rows, offsets = owner_layout(lengths, own_rows)
    positions = offsets + PRE_LEN
    normed = rms_scale(hidden_in, attn_gain).astype(jnp.bfloat16)
    kv_weight = lax.dynamic_index_in_dim(keyval_weight, kv_head, 0, keepdims=False)
    united_weight = jnp.concatenate([query_weight, kv_weight], axis=1)
    projected = jnp.dot(
        lax.all_gather(normed, "tok", axis=0, tiled=True),
        united_weight,
        preferred_element_type=jnp.float32,
    )
    queries = rotate(
        projected[:, : heads_here * HD].reshape(own_rows, heads_here, HD), positions
    ).astype(jnp.bfloat16)
    keyvals = projected[:, heads_here * HD :].reshape(own_rows, 1, 2 * HD)
    rotated = rotate(keyvals[:, :, :HD], positions)
    keyvals = jnp.concatenate([rotated, keyvals[:, :, HD:]], axis=-1).astype(jnp.bfloat16)
    cache_width = kv_count * 2 * HD // tok_count
    cache_offset = tok_place * cache_width % (2 * HD)
    suffix_cache = lax.dynamic_slice_in_dim(keyvals[:, 0, :], cache_offset, cache_width, 1)
    every_owner = lax.all_gather(prefix_cache, "req", axis=0, tiled=True)
    routed = jnp.repeat(every_owner, repeat_count, axis=1)
    windows = lax.all_to_all(routed, "tok", split_axis=1, concat_axis=2, tiled=True)
    windows = windows[:, 0]
    padded_queries = jnp.concatenate(
        [queries, jnp.zeros((most_rows, heads_here, HD), jnp.bfloat16)], axis=0
    )
    padded_keyvals = jnp.concatenate(
        [keyvals, jnp.zeros((most_rows, 1, 2 * HD), jnp.bfloat16)], axis=0
    )
    cache_rows = slot_lookup(prefix_of[0], prefix_slot)

    def one_request(buffer, request):
        first_row, live_len, cache_row = request
        query_block = lax.dynamic_slice_in_dim(padded_queries, first_row, most_rows, 0).reshape(
            most_rows, 1, heads_here, HD
        )
        suffix_block = lax.dynamic_slice_in_dim(padded_keyvals, first_row, most_rows, 0)
        window = lax.dynamic_index_in_dim(windows, cache_row, 0, keepdims=True)
        mixed_rows = request_attention(query_block, suffix_block, window, live_len)
        current = lax.dynamic_slice_in_dim(buffer, first_row, most_rows, 0)
        keep_rows = jnp.arange(most_rows)[:, None] < live_len
        return (
            lax.dynamic_update_slice_in_dim(
                buffer, jnp.where(keep_rows, mixed_rows, current), first_row, 0
            ),
            None,
        )

    buffer = jnp.zeros((own_rows + most_rows, heads_here * HD), jnp.bfloat16)
    buffer, unused = lax.scan(one_request, buffer, (starts, lengths, cache_rows))
    attended = buffer[:own_rows]
    projected_back = lax.psum_scatter(
        jnp.dot(attended, out_weight, preferred_element_type=jnp.float32).astype(jnp.bfloat16),
        "tok",
        scatter_dimension=0,
        tiled=True,
    ).astype(jnp.float32)
    middle = (hidden_in.astype(jnp.float32) + projected_back).astype(jnp.bfloat16)
    mlp_in = rms_scale(middle, mlp_gain).astype(jnp.bfloat16)
    shard_part = lax.all_gather(mlp_in, "req", axis=0, tiled=True)
    gate_proj = jnp.dot(shard_part, gate_weight, preferred_element_type=jnp.float32)
    lifted = jnp.dot(shard_part, up_weight, preferred_element_type=jnp.float32)
    hidden_act = (jax.nn.silu(gate_proj) * lifted).astype(jnp.bfloat16)
    summed = lax.psum_scatter(
        jnp.dot(hidden_act, down_weight, preferred_element_type=jnp.float32).astype(jnp.bfloat16),
        "req",
        scatter_dimension=0,
        tiled=True,
    ).astype(jnp.float32)
    final_state = (middle.astype(jnp.float32) + summed).astype(jnp.bfloat16)
    local_index = jnp.arange(tok_rows) + tok_place * tok_rows
    picker = (local_index[None, :] == (end_rows - 1)[:, None]).astype(jnp.bfloat16)
    picked = jnp.dot(picker, final_state, preferred_element_type=jnp.float32)
    last_rows = lax.psum(picked.astype(jnp.bfloat16), "tok").astype(jnp.float32)
    mean_square = jnp.mean(last_rows * last_rows, axis=-1, keepdims=True)
    spread = jnp.sqrt(mean_square + epsilon)
    final_normed = (
        last_rows * lax.rsqrt(mean_square + epsilon) * final_gain.astype(jnp.float32)
    ).astype(jnp.bfloat16)
    logits = lax.dot_general(
        final_normed, head_weight, (((1,), (1,)), ((), ())), preferred_element_type=jnp.float32
    )
    highest = lax.pmax(jnp.max(logits, axis=-1), "tok")
    summed_exp = lax.psum(jnp.sum(jnp.exp(logits - highest[:, None]), axis=-1), "tok")
    log_total = highest + jnp.log(summed_exp)
    return (final_state, suffix_cache, spread[:, 0][None, :], highest[None, :], log_total[None, :])


def solution(mesh):
    placed = (
        P(("req", "tok"), None),
        P("req", None),
        P("req", None),
        P(),
        P("req", None, "tok", None),
        P(),
        P(None, "tok"),
        P(),
        P("tok", None),
        P(),
        P(None, "req"),
        P(None, "req"),
        P("req", None),
        P(),
        P("tok", None),
    )
    return jax.shard_map(
        shards,
        mesh=mesh,
        in_specs=placed,
        out_specs=(
            P(("req", "tok"), None),
            P("req", "tok"),
            P("req", None),
            P("req", None),
            P("req", None),
        ),
        check_vma=False,
    )
```

profile of v0, /device:TPU:0, one launch (start us, length us, event | category | flops | bytes accessed | tf_op | source)
XLA Modules:
  0.0 462.7 jit_solution(11795564161702369459)
XLA Ops:
  8.7 1.2 fusion.38
  9.9 2.0 fusion.40
  11.9 28.3 %all-gather.4.cloned.1.call-done = bf16[4,4,256,128]{3,2,1,0:T(8,128)(2,1)} async-done(((bf16[1,4,256,128]{3,2,1,0:T(8,128)(2,1)}), bf16[4,4,256,128]{3,2,1,0:T(8,128)(2,1)}) %all-gather.4.cloned.1.call-update) | async-done | bytes 1048592 | tf_op jit(solution)/shard_map/all_gather | solution.py:131
  40.2 1.5 copy.29
  41.8 1.6 broadcast_in_dim.58
  43.4 4.3 all-to-all-start
  50.1 1.2 broadcast_add_fusion
  51.9 29.2 %all-to-all-done = bf16[4,8,256,128]{2,3,0,1:T(8,128)(2,1)} async-done(((bf16[4,8,256,128]{2,3,0,1:T(8,128)(2,1)}), bf16[4,8,256,128]{2,3,0,1:T(8,128)(2,1)}, u32[]{:S(2)}, u32[]{:S(2)}) %all-to-all-start) | async-done | bytes 2097184 | tf_op jit(solution)/shard_map/all_to_all | solution.py:133
  81.1 3.0 copy.30
  84.2 8.7 %all-gather.6.cloned.1.call-done = bf16[1024,2048]{1,0:T(8,128)(2,1)} async-done(((bf16[128,2048]{1,0:T(8,128)(2,1)}), bf16[1024,2048]{1,0:T(8,128)(2,1)}) %all-gather.6.cloned.1.call-update) | async-done | bytes 4194320 | tf_op jit(solution)/shard_map/all_gather | solution.py:118
  92.9 4.3 fusion.34
  99.6 0.9 fusion.46
  100.5 0.9 broadcast_in_dim.55
  101.5 129.9 %while.10 = (s32[]{:T(128)}, bf16[1536,256]{0,1:T(8,128)(2,1)}, s32[4]{0:T(128)}, s32[4]{0:T(128)}, bf16[4,2048,128]{2,1,0:T(8,128)(2,1)S(1)}, /*index=5*/s32[4]...) while((s32[]{:T(128)}, bf16[1536,256]{0,1:T(8,128)(2,1)}, ...), condition=%wide.region_7.8_spmd, body=%wide.region_4.7_spmd.sunk | while | flops 1415707136 | bytes 83556792 | solution.py:161
  101.5 1.2 dynamic_slice.52
  103.4 1.2 dynamic_slice.54
  106.6 1.2 dynamic_slice.53
  109.7 1.0 dynamic-slice_bitcast_fusion.4
  111.7 0.9 copy.38
  113.6 4.7 %fusion.93 = (f32[4,512]{1,0:T(4,128)S(1)}, f32[2560,512,4]{1,0,2:T(8,128)S(1)}) fusion(pred[512,2560]{0,1:T(8,128)(4,1)S(1)} %pad_add_fusion.2, bf16[1536,4,64]{0,2,1:T(8,128)(2,1)} %get-tuple-element.192, s32[]{:T(128)S(6)} %select_n.119, bf16[1,512,64]{1,2,0:T(8,128)(2,1)S(1)} %copy-done.10, bf16[1,2048,64]{1,2,0:T(8,128)(2,1)S(1)} %copy-done.5), kind=kOutput, calls=%fused_computation.2.clone.1 | convolution fusion | flops 687470592 | bytes 22880260 | tf_op jit(solution)/shard_map/while/body/eval_jaxpr/rgke,gse->gkrs/dot_general | solution.py:61
  118.3 5.2 %fusion.94 = f32[4,512]{1,0:T(4,128)S(1)} fusion(f32[2560,512,4]{1,0,2:T(8,128)S(1)} %get-tuple-element.155, f32[4,512]{1,0:T(4,128)S(1)} %get-tuple-element.156, pred[512,2560]{0,1:T(8,128)(4,1)S(1)} %pad_add_fusion.2), kind=kLoop, calls=%fused_computation.3.clone.1 | loop fusion | flops 26212352 | bytes 22298624 | tf_op jit(solution)/shard_map/while/body/eval_jaxpr/reduce_sum | solution.py:75
  123.6 5.9 %fusion.96 = bf16[512,1,4,64]{0,3,2,1:T(8,128)(2,1)S(1)} fusion(f32[2560,512,4]{1,0,2:T(8,128)S(1)} %get-tuple-element.155, f32[4,512]{1,0:T(4,128)S(1)} %get-tuple-element.156, pred[512,2560]{0,1:T(8,128)(4,1)S(1)} %pad_add_fusion.2, bf16[1,512,64]{1,2,0:T(8,128)(2,1)S(1)} %get-tuple-element.157, bf16[1,2048,64]{1,2,0:T(8,128)(2,1)S(1)} %copy.39, ...), kind=kOutput, calls=%fused_computation.17.clone.1 | convolution fusion | flops 698220544 | bytes 22888448 | tf_op jit(solution)/shard_map/while/body/eval_jaxpr/gkrs,gse->rgke/dot_general | solution.py:78
  130.3 2.5 dynamic_update_slice.4
  132.8 0.9 copy-done.4
  133.6 1.2 dynamic_slice.52
  135.5 1.2 dynamic_slice.54
  138.7 1.2 dynamic_slice.53
  141.9 1.0 dynamic-slice_bitcast_fusion.4
  143.9 0.9 copy.38
  145.8 4.7 %fusion.93 = (f32[4,512]{1,0:T(4,128)S(1)}, f32[2560,512,4]{1,0,2:T(8,128)S(1)}) fusion(pred[512,2560]{0,1:T(8,128)(4,1)S(1)} %pad_add_fusion.2, bf16[1536,4,64]{0,2,1:T(8,128)(2,1)} %get-tuple-element.192, s32[]{:T(128)S(6)} %select_n.119, bf16[1,512,64]{1,2,0:T(8,128)(2,1)S(1)} %copy-done.10, bf16[1,2048,64]{1,2,0:T(8,128)(2,1)S(1)} %copy-done.5), kind=kOutput, calls=%fused_computation.2.clone.1 | convolution fusion | flops 687470592 | bytes 22880260 | tf_op jit(solution)/shard_map/while/body/eval_jaxpr/rgke,gse->gkrs/dot_general | solution.py:61
  150.5 5.2 %fusion.94 = f32[4,512]{1,0:T(4,128)S(1)} fusion(f32[2560,512,4]{1,0,2:T(8,128)S(1)} %get-tuple-element.155, f32[4,512]{1,0:T(4,128)S(1)} %get-tuple-element.156, pred[512,2560]{0,1:T(8,128)(4,1)S(1)} %pad_add_fusion.2), kind=kLoop, calls=%fused_computation.3.clone.1 | loop fusion | flops 26212352 | bytes 22298624 | tf_op jit(solution)/shard_map/while/body/eval_jaxpr/reduce_sum | solution.py:75
  155.7 5.9 %fusion.96 = bf16[512,1,4,64]{0,3,2,1:T(8,128)(2,1)S(1)} fusion(f32[2560,512,4]{1,0,2:T(8,128)S(1)} %get-tuple-element.155, f32[4,512]{1,0:T(4,128)S(1)} %get-tuple-element.156, pred[512,2560]{0,1:T(8,128)(4,1)S(1)} %pad_add_fusion.2, bf16[1,512,64]{1,2,0:T(8,128)(2,1)S(1)} %get-tuple-element.157, bf16[1,2048,64]{1,2,0:T(8,128)(2,1)S(1)} %copy.39, ...), kind=kOutput, calls=%fused_computation.17.clone.1 | convolution fusion | flops 698220544 | bytes 22888448 | tf_op jit(solution)/shard_map/while/body/eval_jaxpr/gkrs,gse->rgke/dot_general | solution.py:78
  162.4 3.1 dynamic_update_slice.4
  166.4 1.2 dynamic_slice.52
  168.3 1.2 dynamic_slice.54
  171.5 1.2 dynamic_slice.53
  174.7 1.0 dynamic-slice_bitcast_fusion.4
  176.7 0.9 copy.38
  178.6 4.7 %fusion.93 = (f32[4,512]{1,0:T(4,128)S(1)}, f32[2560,512,4]{1,0,2:T(8,128)S(1)}) fusion(pred[512,2560]{0,1:T(8,128)(4,1)S(1)} %pad_add_fusion.2, bf16[1536,4,64]{0,2,1:T(8,128)(2,1)} %get-tuple-element.192, s32[]{:T(128)S(6)} %select_n.119, bf16[1,512,64]{1,2,0:T(8,128)(2,1)S(1)} %copy-done.10, bf16[1,2048,64]{1,2,0:T(8,128)(2,1)S(1)} %copy-done.5), kind=kOutput, calls=%fused_computation.2.clone.1 | convolution fusion | flops 687470592 | bytes 22880260 | tf_op jit(solution)/shard_map/while/body/eval_jaxpr/rgke,gse->gkrs/dot_general | solution.py:61
  183.3 5.2 %fusion.94 = f32[4,512]{1,0:T(4,128)S(1)} fusion(f32[2560,512,4]{1,0,2:T(8,128)S(1)} %get-tuple-element.155, f32[4,512]{1,0:T(4,128)S(1)} %get-tuple-element.156, pred[512,2560]{0,1:T(8,128)(4,1)S(1)} %pad_add_fusion.2), kind=kLoop, calls=%fused_computation.3.clone.1 | loop fusion | flops 26212352 | bytes 22298624 | tf_op jit(solution)/shard_map/while/body/eval_jaxpr/reduce_sum | solution.py:75
  188.5 5.9 %fusion.96 = bf16[512,1,4,64]{0,3,2,1:T(8,128)(2,1)S(1)} fusion(f32[2560,512,4]{1,0,2:T(8,128)S(1)} %get-tuple-element.155, f32[4,512]{1,0:T(4,128)S(1)} %get-tuple-element.156, pred[512,2560]{0,1:T(8,128)(4,1)S(1)} %pad_add_fusion.2, bf16[1,512,64]{1,2,0:T(8,128)(2,1)S(1)} %get-tuple-element.157, bf16[1,2048,64]{1,2,0:T(8,128)(2,1)S(1)} %copy.39, ...), kind=kOutput, calls=%fused_computation.17.clone.1 | convolution fusion | flops 698220544 | bytes 22888448 | tf_op jit(solution)/shard_map/while/body/eval_jaxpr/gkrs,gse->rgke/dot_general | solution.py:78
  195.2 3.1 dynamic_update_slice.4
  199.2 1.2 dynamic_slice.52
  201.1 1.2 dynamic_slice.54
  204.3 1.2 dynamic_slice.53
  207.5 1.0 dynamic-slice_bitcast_fusion.4
  209.5 0.9 copy.38
  211.4 4.7 %fusion.93 = (f32[4,512]{1,0:T(4,128)S(1)}, f32[2560,512,4]{1,0,2:T(8,128)S(1)}) fusion(pred[512,2560]{0,1:T(8,128)(4,1)S(1)} %pad_add_fusion.2, bf16[1536,4,64]{0,2,1:T(8,128)(2,1)} %get-tuple-element.192, s32[]{:T(128)S(6)} %select_n.119, bf16[1,512,64]{1,2,0:T(8,128)(2,1)S(1)} %copy-done.10, bf16[1,2048,64]{1,2,0:T(8,128)(2,1)S(1)} %copy-done.5), kind=kOutput, calls=%fused_computation.2.clone.1 | convolution fusion | flops 687470592 | bytes 22880260 | tf_op jit(solution)/shard_map/while/body/eval_jaxpr/rgke,gse->gkrs/dot_general | solution.py:61
  216.1 5.2 %fusion.94 = f32[4,512]{1,0:T(4,128)S(1)} fusion(f32[2560,512,4]{1,0,2:T(8,128)S(1)} %get-tuple-element.155, f32[4,512]{1,0:T(4,128)S(1)} %get-tuple-element.156, pred[512,2560]{0,1:T(8,128)(4,1)S(1)} %pad_add_fusion.2), kind=kLoop, calls=%fused_computation.3.clone.1 | loop fusion | flops 26212352 | bytes 22298624 | tf_op jit(solution)/shard_map/while/body/eval_jaxpr/reduce_sum | solution.py:75
  221.3 5.9 %fusion.96 = bf16[512,1,4,64]{0,3,2,1:T(8,128)(2,1)S(1)} fusion(f32[2560,512,4]{1,0,2:T(8,128)S(1)} %get-tuple-element.155, f32[4,512]{1,0:T(4,128)S(1)} %get-tuple-element.156, pred[512,2560]{0,1:T(8,128)(4,1)S(1)} %pad_add_fusion.2, bf16[1,512,64]{1,2,0:T(8,128)(2,1)S(1)} %get-tuple-element.157, bf16[1,2048,64]{1,2,0:T(8,128)(2,1)S(1)} %copy.39, ...), kind=kOutput, calls=%fused_computation.17.clone.1 | convolution fusion | flops 698220544 | bytes 22888448 | tf_op jit(solution)/shard_map/while/body/eval_jaxpr/gkrs,gse->rgke/dot_general | solution.py:78
  228.0 2.5 dynamic_update_slice.4
  231.4 4.7 %convolution_convert_fusion = bf16[1024,2048]{1,0:T(8,128)(2,1)} fusion(bf16[256,2048]{1,0:T(8,128)(2,1)} %param.25, bf16[1536,256]{0,1:T(8,128)(2,1)} %get-tuple-element.47), kind=kOutput, calls=%fused_computation.39 | convolution fusion | flops 1075838976 | bytes 5767168 | tf_op jit(solution)/shard_map/dot_general | solution.py:164
  236.2 49.3 %reduce-scatter.3.cloned.1.call-done = bf16[128,2048]{1,0:T(8,128)(2,1)} async-done(((bf16[1024,2048]{1,0:T(8,128)(2,1)}), bf16[128,2048]{1,0:T(8,128)(2,1)}) %reduce-scatter.3.cloned.1.call-update) | async-done | bytes 524304 | tf_op jit(solution)/shard_map/reduce_scatter | solution.py:163
  285.5 1.3 fusion.42
  286.8 2.0 fusion.44
  288.9 46.0 %all-gather.8.cloned.1.call-done = bf16[512,2048]{1,0:T(8,128)(2,1)} async-done(((bf16[128,2048]{1,0:T(8,128)(2,1)}), bf16[512,2048]{1,0:T(8,128)(2,1)}) %all-gather.8.cloned.1.call-update) | async-done | bytes 2097168 | tf_op jit(solution)/shard_map/all_gather | solution.py:171
  334.9 6.5 %fusion.73 = f32[512,1024]{1,0:T(8,128)} fusion(bf16[512,2048]{1,0:T(8,128)(2,1)} %all-gather.8.cloned.1.call-done, bf16[2048,1024]{1,0:T(8,128)(2,1)} %param.27), kind=kOutput, calls=%fused_computation.120 | convolution fusion | flops 2147483648 | bytes 8388608 | tf_op jit(solution)/shard_map/dot_general | solution.py:172
  341.4 10.6 %convolution_convert_fusion.1 = bf16[512,2048]{1,0:T(8,128)(2,1)} fusion(bf16[1024,2048]{1,0:T(8,128)(2,1)} %param.29, f32[512,1024]{1,0:T(8,128)} %fusion.73, bf16[512,2048]{1,0:T(8,128)(2,1)} %all-gather.8.cloned.1.call-done, bf16[2048,1024]{1,0:T(8,128)(2,1)} %param.28), kind=kOutput, calls=%fused_computation.40 | convolution fusion | flops 4299161600 | bytes 14680064 | tf_op jit(solution)/shard_map/dot_general | solution.py:176
  352.1 42.7 %reduce-scatter.5.cloned.1.call-done = bf16[128,2048]{1,0:T(8,128)(2,1)} async-done(((bf16[512,2048]{1,0:T(8,128)(2,1)}), bf16[128,2048]{1,0:T(8,128)(2,1)}) %reduce-scatter.5.cloned.1.call-update) | async-done | bytes 524304 | tf_op jit(solution)/shard_map/reduce_scatter | solution.py:175
  394.8 1.3 fusion.45
  396.3 23.8 %psum.14 = bf16[4,2048]{1,0:T(4,128)(2,1)S(1)} all-reduce(bf16[4,2048]{1,0:T(4,128)(2,1)S(1)} %convolution_convert_fusion.2), channel_id=1, replica_groups=mesh['req'=4,'tok'=8] {'tok'}, use_global_device_ids=true, to_apply=%region_11.12 | all-reduce | flops 8192 | bytes 32768 | tf_op jit(solution)/shard_map/psum | solution.py:185
  420.8 10.3 %fusion.72 = (f32[4]{0:T(128)S(1)}, f32[4,4000]{1,0:T(4,128)S(1)}) fusion(bf16[4000,2048]{1,0:T(8,128)(2,1)} %param.31, bf16[4,2048]{1,0:T(4,128)(2,1)S(1)} %psum.14, f32[2048]{0:T(1024)S(1)} %convert_element_type.108, f32[4]{0:T(128)S(1)} %get-tuple-element.92), kind=kOutput, calls=%fused_computation.119 | convolution fusion | flops 65584764 | bytes 16472608 | tf_op jit(solution)/shard_map/dot_general | solution.py:191
  431.1 11.8 %pmax.7 = f32[4]{0:T(128)S(1)} all-reduce(f32[4]{0:T(128)S(1)} %get-tuple-element.96), channel_id=1, replica_groups=mesh['req'=4,'tok'=8] {'tok'}, use_global_device_ids=true, to_apply=%region_14.15 | all-reduce | flops 4 | bytes 32 | tf_op jit(solution)/shard_map/pmax | solution.py:194
  443.8 11.8 %psum.15 = f32[4]{0:T(128)S(1)} all-reduce(f32[4]{0:T(128)S(1)} %exponential_reduce_fusion), channel_id=1, replica_groups=mesh['req'=4,'tok'=8] {'tok'}, use_global_device_ids=true, to_apply=%region_16.17 | all-reduce | flops 4 | bytes 32 | tf_op jit(solution)/shard_map/psum | solution.py:195
  (146 shorter events, 25.3 us)
Async XLA Ops:
  7.2 44.7 %copy-start = (bf16[4,2048,128]{2,1,0:T(8,128)(2,1)S(1)}, bf16[4,2048,128]{2,1,0:T(8,128)(2,1)}, u32[]{:S(2)}) copy-start(bf16[4,2048,128]{2,1,0:T(8,128)(2,1)} %param.24) | copy-start | bytes 6291460
  7.2 33.1 %all-gather.4.cloned.1.call-start = ((), (), s32[]{:S(2)}) async-start(), calls=%async_computation.3 | async-start | bytes 1310720 | tf_op jit(solution)/shard_map/all_gather | solution.py:131
  7.9 84.9 %all-gather.6.cloned.1.call-start = ((), (), s32[]{:S(2)}) async-start(), calls=%async_computation.4 | async-start | bytes 4718592 | tf_op jit(solution)/shard_map/all_gather | solution.py:118
  41.7 6.9 %copy-start.17 = (s32[4]{0:T(128)S(1)}, s32[4]{0:T(128)}, u32[]{:S(2)}) copy-start(s32[4]{0:T(128)} %param.20) | copy-start | bytes 52
  41.8 6.9 %copy-start.18 = (s32[1,4]{1,0:T(1,128)S(1)}, s32[1,4]{1,0:T(1,128)}, u32[]{:S(2)}) copy-start(s32[1,4]{1,0:T(1,128)} %param.19) | copy-start | bytes 52
  43.4 37.7 %all-to-all-start = ((bf16[4,8,256,128]{2,3,0,1:T(8,128)(2,1)}), bf16[4,8,256,128]{2,3,0,1:T(8,128)(2,1)}, u32[]{:S(2)}, u32[]{:S(2)}) async-start(bf16[4,8,256,128]{2,3,0,1:T(8,128)(2,1)} %bitcast.128), calls=%async_computation | async-start | bytes 4194304 | tf_op jit(solution)/shard_map/all_to_all | solution.py:133
  47.8 237.7 %reduce-scatter.3.cloned.1.call-start = ((), (), s32[]{:S(2)}) async-start(), calls=%async_computation.5 | async-start | bytes 4718592 | tf_op jit(solution)/shard_map/reduce_scatter | solution.py:163
  97.9 0.7 copy-start.8
  103.4 8.0 %copy-start.11 = (pred[512]{0:T(512)(128)(4,1)}, pred[512]{0:T(512)(128)(4,1)S(1)}, u32[]{:S(2)}) copy-start(pred[512]{0:T(512)(128)(4,1)S(1)} %iota_compare_fusion.9) | copy-start | bytes 1540 | tf_op jit(solution)/shard_map/while
  112.6 1.0 copy-start.5
  112.7 1.0 copy-start.10
  118.3 5.2 %copy-start.12 = (pred[512]{0:T(512)(128)(4,1)S(1)}, pred[512]{0:T(512)(128)(4,1)}, u32[]{:S(2)}) copy-start(pred[512]{0:T(512)(128)(4,1)} %copy-done.11) | copy-start | bytes 1540 | tf_op jit(solution)/shard_map/while
  123.5 5.9 %copy-start.3 = (bf16[1536,256]{0,1:T(8,128)(2,1)S(1)}, bf16[1536,256]{0,1:T(8,128)(2,1)}, u32[]{:S(2)}) copy-start(bf16[1536,256]{0,1:T(8,128)(2,1)} %get-tuple-element.173) | copy-start | bytes 2359300 | tf_op jit(solution)/shard_map/while
  132.8 0.9 copy-start.4
  135.5 8.0 %copy-start.11 = (pred[512]{0:T(512)(128)(4,1)}, pred[512]{0:T(512)(128)(4,1)S(1)}, u32[]{:S(2)}) copy-start(pred[512]{0:T(512)(128)(4,1)S(1)} %iota_compare_fusion.9) | copy-start | bytes 1540 | tf_op jit(solution)/shard_map/while
  144.8 1.0 copy-start.5
  144.8 1.0 copy-start.10
  150.5 5.2 %copy-start.12 = (pred[512]{0:T(512)(128)(4,1)S(1)}, pred[512]{0:T(512)(128)(4,1)}, u32[]{:S(2)}) copy-start(pred[512]{0:T(512)(128)(4,1)} %copy-done.11) | copy-start | bytes 1540 | tf_op jit(solution)/shard_map/while
  155.7 5.9 %copy-start.3 = (bf16[1536,256]{0,1:T(8,128)(2,1)S(1)}, bf16[1536,256]{0,1:T(8,128)(2,1)}, u32[]{:S(2)}) copy-start(bf16[1536,256]{0,1:T(8,128)(2,1)} %get-tuple-element.173) | copy-start | bytes 2359300 | tf_op jit(solution)/shard_map/while
  165.5 0.9 copy-start.4
  168.3 8.0 %copy-start.11 = (pred[512]{0:T(512)(128)(4,1)}, pred[512]{0:T(512)(128)(4,1)S(1)}, u32[]{:S(2)}) copy-start(pred[512]{0:T(512)(128)(4,1)S(1)} %iota_compare_fusion.9) | copy-start | bytes 1540 | tf_op jit(solution)/shard_map/while
  177.6 1.0 copy-start.5
  177.6 1.0 copy-start.10
  183.3 5.2 %copy-start.12 = (pred[512]{0:T(512)(128)(4,1)S(1)}, pred[512]{0:T(512)(128)(4,1)}, u32[]{:S(2)}) copy-start(pred[512]{0:T(512)(128)(4,1)} %copy-done.11) | copy-start | bytes 1540 | tf_op jit(solution)/shard_map/while
  188.5 5.9 %copy-start.3 = (bf16[1536,256]{0,1:T(8,128)(2,1)S(1)}, bf16[1536,256]{0,1:T(8,128)(2,1)}, u32[]{:S(2)}) copy-start(bf16[1536,256]{0,1:T(8,128)(2,1)} %get-tuple-element.173) | copy-start | bytes 2359300 | tf_op jit(solution)/shard_map/while
  198.3 0.9 copy-start.4
  201.1 8.0 %copy-start.11 = (pred[512]{0:T(512)(128)(4,1)}, pred[512]{0:T(512)(128)(4,1)S(1)}, u32[]{:S(2)}) copy-start(pred[512]{0:T(512)(128)(4,1)S(1)} %iota_compare_fusion.9) | copy-start | bytes 1540 | tf_op jit(solution)/shard_map/while
  210.4 1.0 copy-start.5
  210.4 1.0 copy-start.10
  216.1 5.2 %copy-start.12 = (pred[512]{0:T(512)(128)(4,1)S(1)}, pred[512]{0:T(512)(128)(4,1)}, u32[]{:S(2)}) copy-start(pred[512]{0:T(512)(128)(4,1)} %copy-done.11) | copy-start | bytes 1540 | tf_op jit(solution)/shard_map/while
  221.3 5.9 %copy-start.3 = (bf16[1536,256]{0,1:T(8,128)(2,1)S(1)}, bf16[1536,256]{0,1:T(8,128)(2,1)}, u32[]{:S(2)}) copy-start(bf16[1536,256]{0,1:T(8,128)(2,1)} %get-tuple-element.173) | copy-start | bytes 2359300 | tf_op jit(solution)/shard_map/while
  230.5 0.9 copy-start.4
  231.4 4.7 %copy-start.13 = (bf16[2048]{0:T(1024)(128)(2,1)S(1)}, bf16[2048]{0:T(1024)(128)(2,1)}, u32[]{:S(2)}) copy-start(bf16[2048]{0:T(1024)(128)(2,1)} %param.26) | copy-start | bytes 12292
  231.4 54.0 %copy-start.2 = (bf16[128,2048]{1,0:T(8,128)(2,1)S(1)}, bf16[128,2048]{1,0:T(8,128)(2,1)}, u32[]{:S(2)}) copy-start(bf16[128,2048]{1,0:T(8,128)(2,1)} %param.17) | copy-start | bytes 1572868
  236.1 98.8 %all-gather.8.cloned.1.call-start = ((), (), s32[]{:S(2)}) async-start(), calls=%async_computation.6 | async-start | bytes 2621440 | tf_op jit(solution)/shard_map/all_gather | solution.py:171
  288.8 106.0 %reduce-scatter.5.cloned.1.call-start = ((), (), s32[]{:S(2)}) async-start(), calls=%async_computation.7 | async-start | bytes 2621440 | tf_op jit(solution)/shard_map/reduce_scatter | solution.py:175
  341.4 10.7 %copy-start.14 = (bf16[2048]{0:T(1024)(128)(2,1)S(1)}, bf16[2048]{0:T(1024)(128)(2,1)}, u32[]{:S(2)}) copy-start(bf16[2048]{0:T(1024)(128)(2,1)} %param.30) | copy-start | bytes 12292
  341.4 53.4 %copy-start.6 = (bf16[128,2048]{1,0:T(8,128)(2,1)S(1)}, bf16[128,2048]{1,0:T(8,128)(2,1)}, u32[]{:S(2)}) copy-start(bf16[128,2048]{1,0:T(8,128)(2,1)} %reduce-scatter.3.cloned.1.call-done) | copy-start | bytes 1572868
  352.0 44.1 %copy-start.15 = (s32[4]{0:T(128)S(1)}, s32[4]{0:T(128)}, u32[]{:S(2)}) copy-start(s32[4]{0:T(128)} %get-tuple-element.94) | copy-start | bytes 52
  396.1 35.0 %copy-start.7 = (bf16[128,2048]{1,0:T(8,128)(2,1)}, bf16[128,2048]{1,0:T(8,128)(2,1)S(1)}, u32[]{:S(2)}) copy-start(bf16[128,2048]{1,0:T(8,128)(2,1)S(1)} %fusion.45) | copy-start | bytes 1572868
  420.8 22.3 %copy-start.9 = (bf16[1024,1,128]{0,2,1:T(8,128)(2,1)S(1)}, bf16[1024,1,128]{0,2,1:T(8,128)(2,1)}, u32[]{:S(2)}) copy-start(bf16[1024,1,128]{0,2,1:T(8,128)(2,1)} %copy-done.8) | copy-start | bytes 786436
  420.8 35.3 %copy-start.1 = (bf16[4,2048,128]{2,1,0:T(8,128)(2,1)S(1)}, bf16[4,2048,128]{2,1,0:T(8,128)(2,1)}, u32[]{:S(2)}) copy-start(bf16[4,2048,128]{2,1,0:T(8,128)(2,1)} %param.24) | copy-start | bytes 6291460
  442.9 13.2 %copy-start.16 = (f32[4]{0:T(128)}, f32[4]{0:T(128)S(1)}, u32[]{:S(2)}) copy-start(f32[4]{0:T(128)S(1)} %pmax.7) | copy-start | bytes 52
Sparse Core Ops, SparseCore 0:
  9.6 30.6 all-gather.3
  42.7 50.0 all-gather.5
  236.2 49.1 reduce-scatter.2
  289.0 45.9 all-gather.7
  352.2 42.5 reduce-scatter.4
where the time goes:
time: 464 us; the launch traced here: 463 us
  waiting for transfers between devices  205 us (44%)
  matrix products  79 us (17%)
  local copies, waits for them, and re-layouts  50.9 us (11%)
  blocking collectives  47.4 us (10%)
  other arithmetic  45.6 us (10%)
  loops' own time  16.2 us (3%)
  between operations  14 us (3%)
    reduce_scatter x1, waiting for transfers between devices, shards(): lax.psum_scatter(jnp.dot(attended, out_weight, preferred_element_type=jnp...  49.3 us
    all_gather x1, waiting for transfers between devices, shards(): shard_part = lax.all_gather(mlp_in, 'req', axis=0, tiled=True)  46 us
    reduce_scatter x1, waiting for transfers between devices, shards(): lax.psum_scatter(jnp.dot(hidden_act, down_weight, preferred_element_type=...  42.7 us
    all_to_all x1, waiting for transfers between devices, shards(): lax.all_to_all(routed, 'tok', split_axis=1, concat_axis=2, tiled=True)  29.2 us
    all_gather x1, waiting for transfers between devices, shards(): every_owner = lax.all_gather(prefix_cache, 'req', axis=0, tiled=True)  28.3 us
    psum x1, blocking collectives, shards(): last_rows = lax.psum(picked.astype(jnp.bfloat16), 'tok').astype(jnp.float32)  23.8 us
    dot_general x4, matrix products, request_attention(): jnp.einsum('gkrs,gse->rgke', rounded, value_rows, preferred_element_type=...  23.7 us
    reduce_sum x4, other arithmetic, request_attention(): totals = jnp.sum(weights, axis=-1, keepdims=True)  20.8 us
  transfers between devices with their start and end apart: 6, of which 6 were waited for; matrix products, arithmetic and copies ran while one was open for 3% of the time, Pallas kernels for 0%

commit v1 on v0

--- a/solution.py
+++ b/solution.py
@@ -128,7 +128,22 @@
     cache_width = kv_count * 2 * HD // tok_count
     cache_offset = tok_place * cache_width % (2 * HD)
     suffix_cache = lax.dynamic_slice_in_dim(keyvals[:, 0, :], cache_offset, cache_width, 1)
-    every_owner = lax.all_gather(prefix_cache, "req", axis=0, tiled=True)
+    f_now, item_now, res = (lax.psum(1, "req"), lax.axis_index("req"), prefix_cache.shape[0])
+    panels = [dev * f_now if h == 0 else dev for h, dev in enumerate(prefix_cache.shape)]
+    every_owner = lax.dynamic_update_slice_in_dim(
+        jnp.zeros(panels, prefix_cache.dtype), prefix_cache, item_now * res, axis=0
+    )
+    v_now = step_out = prefix_cache
+    for k in range(1, f_now // 2 + 1):
+        v_now = lax.ppermute(v_now, "req", [(h, (h + 1) % f_now) for h in range(f_now)])
+        every_owner = lax.dynamic_update_slice_in_dim(
+            every_owner, v_now, (item_now - k) % f_now * res, axis=0
+        )
+        if 2 * k < f_now:
+            step_out = lax.ppermute(step_out, "req", [(h, (h - 1) % f_now) for h in range(f_now)])
+            every_owner = lax.dynamic_update_slice_in_dim(
+                every_owner, step_out, (item_now + k) % f_now * res, axis=0
+            )
     routed = jnp.repeat(every_owner, repeat_count, axis=1)
     windows = lax.all_to_all(routed, "tok", split_axis=1, concat_axis=2, tiled=True)
     windows = windows[:, 0]

time: 464 us -> 448 us (0.966)
  waiting for transfers between devices: 205 us -> 179 us
  starting transfers between devices: 4.54 us -> 9.68 us
  local copies, waits for them, and re-layouts: 50.9 us -> 55.7 us
    all_gather x1 -> x0, waiting for transfers between devices: 28.3 us -> none  [shards(): every_owner = lax.all_gather(prefix_cache, 'req', axis=0, tiled=True)]
    ppermute x0 -> x3, waiting for transfers between devices: none -> 12.6 us  [the longest x2 9.5 us: shards(): lax.ppermute(v_now, 'req', [(h, (h + 1) % f_now) for h in range(f_now)])]
    all_gather x1, waiting for transfers between devices: 8.7 us -> 0.02 us  [shards(): lax.all_gather(normed, 'tok', axis=0, tiled=True)]
    ppermute x0 -> x3, starting transfers between devices: none -> 5.17 us  [the longest x2 3.08 us: shards(): lax.ppermute(v_now, 'req', [(h, (h + 1) % f_now) for h in range(f_now)])]
  transfers between devices with their start and end apart: 6 -> 8, of which waited for: 6 -> 7; matrix products, arithmetic and copies ran while one was open for 3% -> 3% of each run, Pallas kernels for 0% -> 0%
where the time goes in v1:
time: 448 us; the launch traced here: 446 us
  waiting for transfers between devices  179 us (40%)
  matrix products  79 us (18%)
  local copies, waits for them, and re-layouts  55.7 us (12%)
  blocking collectives  47.4 us (11%)
  other arithmetic  45.7 us (10%)
  loops' own time  16.2 us (4%)
  between operations  14.1 us (3%)
  starting transfers between devices  9.68 us (2%)
    reduce_scatter x1, waiting for transfers between devices, shards(): lax.psum_scatter(jnp.dot(attended, out_weight, preferred_element_type=jnp...  50.1 us
    all_gather x1, waiting for transfers between devices, shards(): shard_part = lax.all_gather(mlp_in, 'req', axis=0, tiled=True)  46 us
    reduce_scatter x1, waiting for transfers between devices, shards(): lax.psum_scatter(jnp.dot(hidden_act, down_weight, preferred_element_type=...  42.7 us
    all_to_all x1, waiting for transfers between devices, shards(): lax.all_to_all(routed, 'tok', split_axis=1, concat_axis=2, tiled=True)  27.1 us
    psum x1, blocking collectives, shards(): last_rows = lax.psum(picked.astype(jnp.bfloat16), 'tok').astype(jnp.float32)  23.8 us
    dot_general x4, matrix products, request_attention(): jnp.einsum('gkrs,gse->rgke', rounded, value_rows, preferred_element_type=...  23.7 us
    reduce_sum x4, other arithmetic, request_attention(): totals = jnp.sum(weights, axis=-1, keepdims=True)  20.8 us
    dot_general x4, matrix products, request_attention(): jnp.einsum('rgke,gse->gkrs', query_block, key_rows, preferred_element_typ...  18.7 us
  transfers between devices with their start and end apart: 8, of which 7 were waited for; matrix products, arithmetic and copies ran while one was open for 3% of the time, Pallas kernels for 0%

profile of v1, /device:TPU:0, one launch (start us, length us, event | category | flops | bytes accessed | tf_op | source)
XLA Modules:
  0.0 446.4 jit_solution(2747676593115399365)
XLA Ops:
  7.2 1.4 fusion.38
  9.3 2.0 fusion.40
  11.3 3.1 collective-permute-start
  14.4 2.1 collective-permute-start.1
  16.5 1.1 copy.38
  17.6 6.3 %collective-permute-done = bf16[1,4,256,128]{3,2,1,0:T(8,128)(2,1)} collective-permute-done((bf16[1,4,256,128]{3,2,1,0:T(8,128)(2,1)}, bf16[1,4,256,128]{3,2,1,0:T(8,128)(2,1)}, u32[]{:S(2)}, u32[]{:S(2)}) %collective-permute-start) | collective-permute-done | bytes 262176 | tf_op jit(solution)/shard_map/ppermute | solution.py:138
  24.1 1.1 copy.39
  25.2 3.1 collective-permute-done.1
  28.3 1.8 copy.40
  30.2 1.0 constant_dynamic-update-slice_fusion.1
  31.2 3.2 collective-permute-done.2
  34.4 1.1 copy.41
  35.5 1.6 broadcast_in_dim.75
  37.1 4.3 all-to-all-start
  43.8 1.2 broadcast_add_fusion
  45.6 27.1 %all-to-all-done = bf16[4,8,256,128]{2,3,0,1:T(8,128)(2,1)} async-done(((bf16[4,8,256,128]{2,3,0,1:T(8,128)(2,1)}), bf16[4,8,256,128]{2,3,0,1:T(8,128)(2,1)}, u32[]{:S(2)}, u32[]{:S(2)}) %all-to-all-start) | async-done | bytes 2097184 | tf_op jit(solution)/shard_map/all_to_all | solution.py:148
  72.7 3.0 copy.42
  75.8 4.3 fusion.34
  84.4 129.9 %while.10 = (s32[]{:T(128)}, bf16[1536,256]{0,1:T(8,128)(2,1)}, s32[4]{0:T(128)}, s32[4]{0:T(128)}, bf16[4,2048,128]{2,1,0:T(8,128)(2,1)S(1)}, /*index=5*/s32[4]...) while((s32[]{:T(128)}, bf16[1536,256]{0,1:T(8,128)(2,1)}, ...), condition=%wide.region_7.8_spmd, body=%wide.region_4.7_spmd.sunk | while | flops 1415707136 | bytes 83556792 | solution.py:176
  84.4 1.2 dynamic_slice.52
  86.3 1.2 dynamic_slice.54
  89.5 1.2 dynamic_slice.53
  92.6 1.0 dynamic-slice_bitcast_fusion.4
  96.6 4.7 %fusion.93 = (f32[4,512]{1,0:T(4,128)S(1)}, f32[2560,512,4]{1,0,2:T(8,128)S(1)}) fusion(pred[512,2560]{0,1:T(8,128)(4,1)S(1)} %pad_add_fusion.2, bf16[1536,4,64]{0,2,1:T(8,128)(2,1)} %get-tuple-element.192, s32[]{:T(128)S(6)} %select_n.150, bf16[1,512,64]{1,2,0:T(8,128)(2,1)S(1)} %copy-done.10, bf16[1,2048,64]{1,2,0:T(8,128)(2,1)S(1)} %copy-done.5), kind=kOutput, calls=%fused_computation.2.clone.1 | convolution fusion | flops 687470592 | bytes 22880260 | tf_op jit(solution)/shard_map/while/body/eval_jaxpr/rgke,gse->gkrs/dot_general | solution.py:61
  101.3 5.2 %fusion.94 = f32[4,512]{1,0:T(4,128)S(1)} fusion(f32[2560,512,4]{1,0,2:T(8,128)S(1)} %get-tuple-element.155, f32[4,512]{1,0:T(4,128)S(1)} %get-tuple-element.156, pred[512,2560]{0,1:T(8,128)(4,1)S(1)} %pad_add_fusion.2), kind=kLoop, calls=%fused_computation.3.clone.1 | loop fusion | flops 26212352 | bytes 22298624 | tf_op jit(solution)/shard_map/while/body/eval_jaxpr/reduce_sum | solution.py:75
  106.5 5.9 %fusion.96 = bf16[512,1,4,64]{0,3,2,1:T(8,128)(2,1)S(1)} fusion(f32[2560,512,4]{1,0,2:T(8,128)S(1)} %get-tuple-element.155, f32[4,512]{1,0:T(4,128)S(1)} %get-tuple-element.156, pred[512,2560]{0,1:T(8,128)(4,1)S(1)} %pad_add_fusion.2, bf16[1,512,64]{1,2,0:T(8,128)(2,1)S(1)} %get-tuple-element.157, bf16[1,2048,64]{1,2,0:T(8,128)(2,1)S(1)} %copy.51, ...), kind=kOutput, calls=%fused_computation.17.clone.1 | convolution fusion | flops 698220544 | bytes 22888448 | tf_op jit(solution)/shard_map/while/body/eval_jaxpr/gkrs,gse->rgke/dot_general | solution.py:78
  113.2 2.5 dynamic_update_slice.24
  116.6 1.2 dynamic_slice.52
  118.5 1.2 dynamic_slice.54
  121.7 1.2 dynamic_slice.53
  124.8 1.0 dynamic-slice_bitcast_fusion.4
  128.7 4.7 %fusion.93 = (f32[4,512]{1,0:T(4,128)S(1)}, f32[2560,512,4]{1,0,2:T(8,128)S(1)}) fusion(pred[512,2560]{0,1:T(8,128)(4,1)S(1)} %pad_add_fusion.2, bf16[1536,4,64]{0,2,1:T(8,128)(2,1)} %get-tuple-element.192, s32[]{:T(128)S(6)} %select_n.150, bf16[1,512,64]{1,2,0:T(8,128)(2,1)S(1)} %copy-done.10, bf16[1,2048,64]{1,2,0:T(8,128)(2,1)S(1)} %copy-done.5), kind=kOutput, calls=%fused_computation.2.clone.1 | convolution fusion | flops 687470592 | bytes 22880260 | tf_op jit(solution)/shard_map/while/body/eval_jaxpr/rgke,gse->gkrs/dot_general | solution.py:61
  133.4 5.2 %fusion.94 = f32[4,512]{1,0:T(4,128)S(1)} fusion(f32[2560,512,4]{1,0,2:T(8,128)S(1)} %get-tuple-element.155, f32[4,512]{1,0:T(4,128)S(1)} %get-tuple-element.156, pred[512,2560]{0,1:T(8,128)(4,1)S(1)} %pad_add_fusion.2), kind=kLoop, calls=%fused_computation.3.clone.1 | loop fusion | flops 26212352 | bytes 22298624 | tf_op jit(solution)/shard_map/while/body/eval_jaxpr/reduce_sum | solution.py:75
  138.7 5.9 %fusion.96 = bf16[512,1,4,64]{0,3,2,1:T(8,128)(2,1)S(1)} fusion(f32[2560,512,4]{1,0,2:T(8,128)S(1)} %get-tuple-element.155, f32[4,512]{1,0:T(4,128)S(1)} %get-tuple-element.156, pred[512,2560]{0,1:T(8,128)(4,1)S(1)} %pad_add_fusion.2, bf16[1,512,64]{1,2,0:T(8,128)(2,1)S(1)} %get-tuple-element.157, bf16[1,2048,64]{1,2,0:T(8,128)(2,1)S(1)} %copy.51, ...), kind=kOutput, calls=%fused_computation.17.clone.1 | convolution fusion | flops 698220544 | bytes 22888448 | tf_op jit(solution)/shard_map/while/body/eval_jaxpr/gkrs,gse->rgke/dot_general | solution.py:78
  145.4 3.1 dynamic_update_slice.24
  149.4 1.2 dynamic_slice.52
  151.3 1.2 dynamic_slice.54
  154.5 1.2 dynamic_slice.53
  157.6 1.0 dynamic-slice_bitcast_fusion.4
  161.5 4.7 %fusion.93 = (f32[4,512]{1,0:T(4,128)S(1)}, f32[2560,512,4]{1,0,2:T(8,128)S(1)}) fusion(pred[512,2560]{0,1:T(8,128)(4,1)S(1)} %pad_add_fusion.2, bf16[1536,4,64]{0,2,1:T(8,128)(2,1)} %get-tuple-element.192, s32[]{:T(128)S(6)} %select_n.150, bf16[1,512,64]{1,2,0:T(8,128)(2,1)S(1)} %copy-done.10, bf16[1,2048,64]{1,2,0:T(8,128)(2,1)S(1)} %copy-done.5), kind=kOutput, calls=%fused_computation.2.clone.1 | convolution fusion | flops 687470592 | bytes 22880260 | tf_op jit(solution)/shard_map/while/body/eval_jaxpr/rgke,gse->gkrs/dot_general | solution.py:61
  166.2 5.2 %fusion.94 = f32[4,512]{1,0:T(4,128)S(1)} fusion(f32[2560,512,4]{1,0,2:T(8,128)S(1)} %get-tuple-element.155, f32[4,512]{1,0:T(4,128)S(1)} %get-tuple-element.156, pred[512,2560]{0,1:T(8,128)(4,1)S(1)} %pad_add_fusion.2), kind=kLoop, calls=%fused_computation.3.clone.1 | loop fusion | flops 26212352 | bytes 22298624 | tf_op jit(solution)/shard_map/while/body/eval_jaxpr/reduce_sum | solution.py:75
  171.5 5.9 %fusion.96 = bf16[512,1,4,64]{0,3,2,1:T(8,128)(2,1)S(1)} fusion(f32[2560,512,4]{1,0,2:T(8,128)S(1)} %get-tuple-element.155, f32[4,512]{1,0:T(4,128)S(1)} %get-tuple-element.156, pred[512,2560]{0,1:T(8,128)(4,1)S(1)} %pad_add_fusion.2, bf16[1,512,64]{1,2,0:T(8,128)(2,1)S(1)} %get-tuple-element.157, bf16[1,2048,64]{1,2,0:T(8,128)(2,1)S(1)} %copy.51, ...), kind=kOutput, calls=%fused_computation.17.clone.1 | convolution fusion | flops 698220544 | bytes 22888448 | tf_op jit(solution)/shard_map/while/body/eval_jaxpr/gkrs,gse->rgke/dot_general | solution.py:78
  178.2 3.1 dynamic_update_slice.24
  182.2 1.2 dynamic_slice.52
  184.1 1.2 dynamic_slice.54
  187.3 1.2 dynamic_slice.53
  190.4 1.0 dynamic-slice_bitcast_fusion.4
  194.3 4.7 %fusion.93 = (f32[4,512]{1,0:T(4,128)S(1)}, f32[2560,512,4]{1,0,2:T(8,128)S(1)}) fusion(pred[512,2560]{0,1:T(8,128)(4,1)S(1)} %pad_add_fusion.2, bf16[1536,4,64]{0,2,1:T(8,128)(2,1)} %get-tuple-element.192, s32[]{:T(128)S(6)} %select_n.150, bf16[1,512,64]{1,2,0:T(8,128)(2,1)S(1)} %copy-done.10, bf16[1,2048,64]{1,2,0:T(8,128)(2,1)S(1)} %copy-done.5), kind=kOutput, calls=%fused_computation.2.clone.1 | convolution fusion | flops 687470592 | bytes 22880260 | tf_op jit(solution)/shard_map/while/body/eval_jaxpr/rgke,gse->gkrs/dot_general | solution.py:61
  199.0 5.2 %fusion.94 = f32[4,512]{1,0:T(4,128)S(1)} fusion(f32[2560,512,4]{1,0,2:T(8,128)S(1)} %get-tuple-element.155, f32[4,512]{1,0:T(4,128)S(1)} %get-tuple-element.156, pred[512,2560]{0,1:T(8,128)(4,1)S(1)} %pad_add_fusion.2), kind=kLoop, calls=%fused_computation.3.clone.1 | loop fusion | flops 26212352 | bytes 22298624 | tf_op jit(solution)/shard_map/while/body/eval_jaxpr/reduce_sum | solution.py:75
  204.3 5.9 %fusion.96 = bf16[512,1,4,64]{0,3,2,1:T(8,128)(2,1)S(1)} fusion(f32[2560,512,4]{1,0,2:T(8,128)S(1)} %get-tuple-element.155, f32[4,512]{1,0:T(4,128)S(1)} %get-tuple-element.156, pred[512,2560]{0,1:T(8,128)(4,1)S(1)} %pad_add_fusion.2, bf16[1,512,64]{1,2,0:T(8,128)(2,1)S(1)} %get-tuple-element.157, bf16[1,2048,64]{1,2,0:T(8,128)(2,1)S(1)} %copy.51, ...), kind=kOutput, calls=%fused_computation.17.clone.1 | convolution fusion | flops 698220544 | bytes 22888448 | tf_op jit(solution)/shard_map/while/body/eval_jaxpr/gkrs,gse->rgke/dot_general | solution.py:78
  211.0 2.5 dynamic_update_slice.24
  214.4 4.7 %convolution_convert_fusion = bf16[1024,2048]{1,0:T(8,128)(2,1)} fusion(bf16[256,2048]{1,0:T(8,128)(2,1)} %param.25, bf16[1536,256]{0,1:T(8,128)(2,1)} %get-tuple-element.47), kind=kOutput, calls=%fused_computation.39 | convolution fusion | flops 1075838976 | bytes 5767168 | tf_op jit(solution)/shard_map/dot_general | solution.py:179
  219.1 50.1 %reduce-scatter.3.cloned.1.call-done = bf16[128,2048]{1,0:T(8,128)(2,1)} async-done(((bf16[1024,2048]{1,0:T(8,128)(2,1)}), bf16[128,2048]{1,0:T(8,128)(2,1)}) %reduce-scatter.3.cloned.1.call-update) | async-done | bytes 524304 | tf_op jit(solution)/shard_map/reduce_scatter | solution.py:178
  269.2 1.3 fusion.42
  270.5 2.0 fusion.44
  272.6 46.0 %all-gather.5.cloned.1.call-done = bf16[512,2048]{1,0:T(8,128)(2,1)} async-done(((bf16[128,2048]{1,0:T(8,128)(2,1)}), bf16[512,2048]{1,0:T(8,128)(2,1)}) %all-gather.5.cloned.1.call-update) | async-done | bytes 2097168 | tf_op jit(solution)/shard_map/all_gather | solution.py:186
  318.7 6.5 %fusion.73 = f32[512,1024]{1,0:T(8,128)} fusion(bf16[512,2048]{1,0:T(8,128)(2,1)} %all-gather.5.cloned.1.call-done, bf16[2048,1024]{1,0:T(8,128)(2,1)} %param.27), kind=kOutput, calls=%fused_computation.124 | convolution fusion | flops 2147483648 | bytes 8388608 | tf_op jit(solution)/shard_map/dot_general | solution.py:187
  325.1 10.6 %convolution_convert_fusion.1 = bf16[512,2048]{1,0:T(8,128)(2,1)} fusion(bf16[1024,2048]{1,0:T(8,128)(2,1)} %param.29, f32[512,1024]{1,0:T(8,128)} %fusion.73, bf16[512,2048]{1,0:T(8,128)(2,1)} %all-gather.5.cloned.1.call-done, bf16[2048,1024]{1,0:T(8,128)(2,1)} %param.28), kind=kOutput, calls=%fused_computation.40 | convolution fusion | flops 4299161600 | bytes 14680064 | tf_op jit(solution)/shard_map/dot_general | solution.py:191
  335.9 42.7 %reduce-scatter.5.cloned.1.call-done = bf16[128,2048]{1,0:T(8,128)(2,1)} async-done(((bf16[512,2048]{1,0:T(8,128)(2,1)}), bf16[128,2048]{1,0:T(8,128)(2,1)}) %reduce-scatter.5.cloned.1.call-update) | async-done | bytes 524304 | tf_op jit(solution)/shard_map/reduce_scatter | solution.py:190
  378.5 1.3 fusion.45
  380.1 23.8 %psum.14 = bf16[4,2048]{1,0:T(4,128)(2,1)S(1)} all-reduce(bf16[4,2048]{1,0:T(4,128)(2,1)S(1)} %convolution_convert_fusion.2), channel_id=1, replica_groups=mesh['req'=4,'tok'=8] {'tok'}, use_global_device_ids=true, to_apply=%region_11.12 | all-reduce | flops 8192 | bytes 32768 | tf_op jit(solution)/shard_map/psum | solution.py:200
  404.6 10.3 %fusion.72 = (f32[4]{0:T(128)S(1)}, f32[4,4000]{1,0:T(4,128)S(1)}) fusion(bf16[4000,2048]{1,0:T(8,128)(2,1)} %param.31, bf16[4,2048]{1,0:T(4,128)(2,1)S(1)} %psum.14, f32[2048]{0:T(1024)S(1)} %convert_element_type.108, f32[4]{0:T(128)S(1)} %get-tuple-element.92), kind=kOutput, calls=%fused_computation.123 | convolution fusion | flops 65584764 | bytes 16472608 | tf_op jit(solution)/shard_map/dot_general | solution.py:206
  414.9 11.8 %pmax.7 = f32[4]{0:T(128)S(1)} all-reduce(f32[4]{0:T(128)S(1)} %get-tuple-element.96), channel_id=1, replica_groups=mesh['req'=4,'tok'=8] {'tok'}, use_global_device_ids=true, to_apply=%region_14.15 | all-reduce | flops 4 | bytes 32 | tf_op jit(solution)/shard_map/pmax | solution.py:209
  427.6 11.8 %psum.15 = f32[4]{0:T(128)S(1)} all-reduce(f32[4]{0:T(128)S(1)} %exponential_reduce_fusion), channel_id=1, replica_groups=mesh['req'=4,'tok'=8] {'tok'}, use_global_device_ids=true, to_apply=%region_16.17 | all-reduce | flops 4 | bytes 32 | tf_op jit(solution)/shard_map/psum | solution.py:210
  (157 shorter events, 31.1 us)
Async XLA Ops:
  7.2 38.4 %copy-start = (bf16[4,2048,128]{2,1,0:T(8,128)(2,1)S(1)}, bf16[4,2048,128]{2,1,0:T(8,128)(2,1)}, u32[]{:S(2)}) copy-start(bf16[4,2048,128]{2,1,0:T(8,128)(2,1)} %param.24) | copy-start | bytes 6291460
  7.2 68.6 %all-gather.3.cloned.1.call-start = ((), (), s32[]{:S(2)}) async-start(), calls=%async_computation.3 | async-start | bytes 4718592 | tf_op jit(solution)/shard_map/all_gather | solution.py:118
  11.3 12.6 %collective-permute-start = (bf16[1,4,256,128]{3,2,1,0:T(8,128)(2,1)}, bf16[1,4,256,128]{3,2,1,0:T(8,128)(2,1)}, u32[]{:S(2)}, u32[]{:S(2)}) collective-permute-start(bf16[1,4,256,128]{3,2,1,0:T(8,128)(2,1)} %param.21), channel_id=1, source_target_pairs={{0,8},{8,16},{16,24},{24,0},{1,9},{9,17},{17,25},{25,1},{2,10},{10... | collective-permute-start | bytes 786440 | tf_op jit(solution)/shard_map/ppermute | solution.py:138
  14.4 13.9 %collective-permute-start.1 = (bf16[1,4,256,128]{3,2,1,0:T(8,128)(2,1)}, bf16[1,4,256,128]{3,2,1,0:T(8,128)(2,1)}, u32[]{:S(2)}, u32[]{:S(2)}) collective-permute-start(bf16[1,4,256,128]{3,2,1,0:T(8,128)(2,1)} %param.21), channel_id=1, source_target_pairs={{0,24},{8,0},{16,8},{24,16},{1,25},{9,1},{17,9},{25,17},{2,26},{10... | collective-permute-start | bytes 786440 | tf_op jit(solution)/shard_map/ppermute | solution.py:143
  23.9 10.4 %collective-permute-start.2 = (bf16[1,4,256,128]{3,2,1,0:T(8,128)(2,1)}, bf16[1,4,256,128]{3,2,1,0:T(8,128)(2,1)}, u32[]{:S(2)}, u32[]{:S(2)}) collective-permute-start(bf16[1,4,256,128]{3,2,1,0:T(8,128)(2,1)} %collective-permute-done), channel_id=1, source_target_pairs={{0,8},{8,16},{16,24},{24,0},{1,9},{9,17},{17,25},{25,1},{2,10},{10... | collective-permute-start | bytes 786440 | tf_op jit(solution)/shard_map/ppermute | solution.py:138
  31.1 11.2 %copy-start.17 = (s32[4]{0:T(128)S(1)}, s32[4]{0:T(128)}, u32[]{:S(2)}) copy-start(s32[4]{0:T(128)} %param.20) | copy-start | bytes 52
  31.1 11.2 %copy-start.18 = (s32[1,4]{1,0:T(1,128)S(1)}, s32[1,4]{1,0:T(1,128)}, u32[]{:S(2)}) copy-start(s32[1,4]{1,0:T(1,128)} %param.19) | copy-start | bytes 52
  37.1 35.6 %all-to-all-start = ((bf16[4,8,256,128]{2,3,0,1:T(8,128)(2,1)}), bf16[4,8,256,128]{2,3,0,1:T(8,128)(2,1)}, u32[]{:S(2)}, u32[]{:S(2)}) async-start(bf16[4,8,256,128]{2,3,0,1:T(8,128)(2,1)} %bitcast.128), calls=%async_computation | async-start | bytes 4194304 | tf_op jit(solution)/shard_map/all_to_all | solution.py:148
  41.5 227.7 %reduce-scatter.3.cloned.1.call-start = ((), (), s32[]{:S(2)}) async-start(), calls=%async_computation.4 | async-start | bytes 4718592 | tf_op jit(solution)/shard_map/reduce_scatter | solution.py:178
  80.9 0.7 copy-start.8
  86.3 8.0 %copy-start.11 = (pred[512]{0:T(512)(128)(4,1)}, pred[512]{0:T(512)(128)(4,1)S(1)}, u32[]{:S(2)}) copy-start(pred[512]{0:T(512)(128)(4,1)S(1)} %iota_compare_fusion.9) | copy-start | bytes 1540 | tf_op jit(solution)/shard_map/while
  95.6 1.0 copy-start.5
  95.6 1.0 copy-start.10
  101.2 5.2 %copy-start.12 = (pred[512]{0:T(512)(128)(4,1)S(1)}, pred[512]{0:T(512)(128)(4,1)}, u32[]{:S(2)}) copy-start(pred[512]{0:T(512)(128)(4,1)} %copy-done.11) | copy-start | bytes 1540 | tf_op jit(solution)/shard_map/while
  106.5 5.9 %copy-start.3 = (bf16[1536,256]{0,1:T(8,128)(2,1)S(1)}, bf16[1536,256]{0,1:T(8,128)(2,1)}, u32[]{:S(2)}) copy-start(bf16[1536,256]{0,1:T(8,128)(2,1)} %get-tuple-element.173) | copy-start | bytes 2359300 | tf_op jit(solution)/shard_map/while
  115.7 0.9 copy-start.4
  118.5 8.0 %copy-start.11 = (pred[512]{0:T(512)(128)(4,1)}, pred[512]{0:T(512)(128)(4,1)S(1)}, u32[]{:S(2)}) copy-start(pred[512]{0:T(512)(128)(4,1)S(1)} %iota_compare_fusion.9) | copy-start | bytes 1540 | tf_op jit(solution)/shard_map/while
  127.8 1.0 copy-start.5
  127.8 1.0 copy-start.10
  133.4 5.2 %copy-start.12 = (pred[512]{0:T(512)(128)(4,1)S(1)}, pred[512]{0:T(512)(128)(4,1)}, u32[]{:S(2)}) copy-start(pred[512]{0:T(512)(128)(4,1)} %copy-done.11) | copy-start | bytes 1540 | tf_op jit(solution)/shard_map/while
  138.7 5.9 %copy-start.3 = (bf16[1536,256]{0,1:T(8,128)(2,1)S(1)}, bf16[1536,256]{0,1:T(8,128)(2,1)}, u32[]{:S(2)}) copy-start(bf16[1536,256]{0,1:T(8,128)(2,1)} %get-tuple-element.173) | copy-start | bytes 2359300 | tf_op jit(solution)/shard_map/while
  148.5 0.9 copy-start.4
  151.3 8.0 %copy-start.11 = (pred[512]{0:T(512)(128)(4,1)}, pred[512]{0:T(512)(128)(4,1)S(1)}, u32[]{:S(2)}) copy-start(pred[512]{0:T(512)(128)(4,1)S(1)} %iota_compare_fusion.9) | copy-start | bytes 1540 | tf_op jit(solution)/shard_map/while
  160.6 1.0 copy-start.5
  160.6 1.0 copy-start.10
  166.2 5.2 %copy-start.12 = (pred[512]{0:T(512)(128)(4,1)S(1)}, pred[512]{0:T(512)(128)(4,1)}, u32[]{:S(2)}) copy-start(pred[512]{0:T(512)(128)(4,1)} %copy-done.11) | copy-start | bytes 1540 | tf_op jit(solution)/shard_map/while
  171.5 5.9 %copy-start.3 = (bf16[1536,256]{0,1:T(8,128)(2,1)S(1)}, bf16[1536,256]{0,1:T(8,128)(2,1)}, u32[]{:S(2)}) copy-start(bf16[1536,256]{0,1:T(8,128)(2,1)} %get-tuple-element.173) | copy-start | bytes 2359300 | tf_op jit(solution)/shard_map/while
  181.3 0.9 copy-start.4
  184.1 8.0 %copy-start.11 = (pred[512]{0:T(512)(128)(4,1)}, pred[512]{0:T(512)(128)(4,1)S(1)}, u32[]{:S(2)}) copy-start(pred[512]{0:T(512)(128)(4,1)S(1)} %iota_compare_fusion.9) | copy-start | bytes 1540 | tf_op jit(solution)/shard_map/while
  193.4 1.0 copy-start.5
  193.4 1.0 copy-start.10
  199.0 5.2 %copy-start.12 = (pred[512]{0:T(512)(128)(4,1)S(1)}, pred[512]{0:T(512)(128)(4,1)}, u32[]{:S(2)}) copy-start(pred[512]{0:T(512)(128)(4,1)} %copy-done.11) | copy-start | bytes 1540 | tf_op jit(solution)/shard_map/while
  204.3 5.9 %copy-start.3 = (bf16[1536,256]{0,1:T(8,128)(2,1)S(1)}, bf16[1536,256]{0,1:T(8,128)(2,1)}, u32[]{:S(2)}) copy-start(bf16[1536,256]{0,1:T(8,128)(2,1)} %get-tuple-element.173) | copy-start | bytes 2359300 | tf_op jit(solution)/shard_map/while
  213.5 0.9 copy-start.4
  214.4 4.7 %copy-start.13 = (bf16[2048]{0:T(1024)(128)(2,1)S(1)}, bf16[2048]{0:T(1024)(128)(2,1)}, u32[]{:S(2)}) copy-start(bf16[2048]{0:T(1024)(128)(2,1)} %param.26) | copy-start | bytes 12292
  214.4 54.9 %copy-start.2 = (bf16[128,2048]{1,0:T(8,128)(2,1)S(1)}, bf16[128,2048]{1,0:T(8,128)(2,1)}, u32[]{:S(2)}) copy-start(bf16[128,2048]{1,0:T(8,128)(2,1)} %param.17) | copy-start | bytes 1572868
  219.1 99.6 %all-gather.5.cloned.1.call-start = ((), (), s32[]{:S(2)}) async-start(), calls=%async_computation.5 | async-start | bytes 2621440 | tf_op jit(solution)/shard_map/all_gather | solution.py:186
  272.6 106.0 %reduce-scatter.5.cloned.1.call-start = ((), (), s32[]{:S(2)}) async-start(), calls=%async_computation.6 | async-start | bytes 2621440 | tf_op jit(solution)/shard_map/reduce_scatter | solution.py:190
  325.1 10.7 %copy-start.14 = (bf16[2048]{0:T(1024)(128)(2,1)S(1)}, bf16[2048]{0:T(1024)(128)(2,1)}, u32[]{:S(2)}) copy-start(bf16[2048]{0:T(1024)(128)(2,1)} %param.30) | copy-start | bytes 12292
  325.1 53.4 %copy-start.6 = (bf16[128,2048]{1,0:T(8,128)(2,1)S(1)}, bf16[128,2048]{1,0:T(8,128)(2,1)}, u32[]{:S(2)}) copy-start(bf16[128,2048]{1,0:T(8,128)(2,1)} %reduce-scatter.3.cloned.1.call-done) | copy-start | bytes 1572868
  335.8 44.1 %copy-start.15 = (s32[4]{0:T(128)S(1)}, s32[4]{0:T(128)}, u32[]{:S(2)}) copy-start(s32[4]{0:T(128)} %get-tuple-element.94) | copy-start | bytes 52
  379.8 35.0 %copy-start.7 = (bf16[128,2048]{1,0:T(8,128)(2,1)}, bf16[128,2048]{1,0:T(8,128)(2,1)S(1)}, u32[]{:S(2)}) copy-start(bf16[128,2048]{1,0:T(8,128)(2,1)S(1)} %fusion.45) | copy-start | bytes 1572868
  404.6 22.3 %copy-start.9 = (bf16[1024,1,128]{0,2,1:T(8,128)(2,1)S(1)}, bf16[1024,1,128]{0,2,1:T(8,128)(2,1)}, u32[]{:S(2)}) copy-start(bf16[1024,1,128]{0,2,1:T(8,128)(2,1)} %copy-done.8) | copy-start | bytes 786436
  404.6 35.3 %copy-start.1 = (bf16[4,2048,128]{2,1,0:T(8,128)(2,1)S(1)}, bf16[4,2048,128]{2,1,0:T(8,128)(2,1)}, u32[]{:S(2)}) copy-start(bf16[4,2048,128]{2,1,0:T(8,128)(2,1)} %param.24) | copy-start | bytes 6291460
  426.7 13.2 %copy-start.16 = (f32[4]{0:T(128)}, f32[4]{0:T(128)S(1)}, u32[]{:S(2)}) copy-start(f32[4]{0:T(128)S(1)} %pmax.7) | copy-start | bytes 52
Sparse Core Ops, SparseCore 0:
  11.5 44.0 all-gather.2
  219.2 49.9 reduce-scatter.2
  272.7 45.9 all-gather.4
  335.9 42.5 reduce-scatter.4
